TPU v7x, 512 devices: a whole 4x8x8 slice. The times are simulated.
512 devices in a mesh: seq: 128 (over x, y_hi, z, core), tp: 4 (over y_lo).
Axes of the slice: x: 4, y: 8 (y_hi: 2, y_lo: 4; y = y_hi * 4 + y_lo), z: 8, core: 2. Of those that a mesh axis runs over, the one named last changes fastest.
Arguments:
- tokens: bfloat16 [16384, 2560], P('seq', 'tp'), may hold values from -6 to 6
- seg_ids: int32 [16384], P('seq'), may hold values from 0 to 31, never falling along the last dimension, each value on 1 to 4096 neighbouring positions
- norm_gain: bfloat16 [2560], replicated, may hold values from 0.099609375 to 1.8984375
- w_query: bfloat16 [2560, 2048], P('seq', 'tp'), may hold values from -3 to 3
- w_keyval: bfloat16 [2560, 512], P('seq'), may hold values from -1 to 1
- w_out: bfloat16 [2048, 2560], P('tp', 'seq'), may hold values from -0.125 to 0.125
Outputs:
- hidden: bfloat16 [16384, 2560], P('seq', 'tp')
- kv_cache: bfloat16 [16384, 512], P('seq')
Inputs may be any that keep to these rules, and one draw needn't show every extreme that they name: `seg_ids`: ids never fall along the stream; each of the 32 requests holds 1 to 4096 consecutive tokens, one exactly 4096.
All inputs are finite; a program needn't handle non-finite values.
Results may differ from a plain program's by a relative error of at most 0.0085.
Values may be sent and summed in bfloat16 or wider, within the bound.
No kernel may reach another device: no remote copies, remote signals or barrier semaphores. Data moves between devices by JAX's collectives and lax.ppermute only.
A program may use at most 64 MiB of HBM per device.

v0:
```python
import jax
import jax.numpy as jnp
from jax import lax
from jax.sharding import PartitionSpec as P

HD = 256
WINDOW = 2048
SEG_MEAN = 512


def from_behind(x, axis, by):
    devices = lax.axis_size(axis)
    pairs = [(i, i + by) for i in range(devices) if 0 <= i + by < devices]
    return lax.ppermute(x, axis, pairs)


def rms_norm(values, gain):
    wide = values.astype(jnp.float32)
    scaled = wide * lax.rsqrt(jnp.mean(wide * wide, axis=-1, keepdims=True) + 1e-06)
    return (scaled * gain.astype(jnp.float32)).astype(jnp.bfloat16)


def rotate(tensor, positions):
    quarter = tensor.shape[-1] // 4
    freq = 10000.0 ** (-jnp.arange(quarter, dtype=jnp.float32) / quarter)
    angle = positions[:, None, None] * freq
    cosine = jnp.cos(angle)
    sine = jnp.sin(angle)
    first = tensor[..., :quarter]
    second = tensor[..., quarter : 2 * quarter]
    return jnp.concatenate(
        [
            first * cosine - second * sine,
            second * cosine + first * sine,
            tensor[..., 2 * quarter :],
        ],
        axis=-1,
    )


def per_device(tokens, seg_ids, norm_gain, w_query, w_keyval, w_out):
    tok_rows = tokens.shape[0]
    seq_count = lax.axis_size("seq")
    my_index = lax.axis_index("seq")
    gathered = lax.all_gather(tokens, "tp", axis=1, tiled=True)
    normed = rms_norm(gathered, norm_gain)
    seg_total = tok_rows * seq_count // SEG_MEAN
    labels = jnp.arange(seg_total, dtype=jnp.int32)
    below = jnp.sum((seg_ids[None, :] < labels[:, None]).astype(jnp.int32), axis=1)
    starts = lax.psum(below, "seq")
    own_start = jnp.sum(jnp.where(seg_ids[:, None] == labels[None, :], starts[None, :], 0), axis=1)
    token_index = my_index * tok_rows + jnp.arange(tok_rows, dtype=jnp.int32)
    positions = (token_index - own_start).astype(jnp.float32)
    query_raw = jnp.dot(
        normed,
        lax.all_gather(w_query, "seq", axis=0, tiled=True),
        preferred_element_type=jnp.float32,
    )
    keyval_raw = jnp.dot(
        normed,
        lax.all_gather(w_keyval, "seq", axis=0, tiled=True),
        preferred_element_type=jnp.float32,
    )
    local_heads = w_query.shape[1] // HD
    queries = rotate(query_raw.reshape(tok_rows, local_heads, HD), positions).astype(jnp.bfloat16)
    key_rows = rotate(keyval_raw[:, None, :HD], positions)[:, 0, :]
    kv_cache = jnp.concatenate([key_rows, keyval_raw[:, HD:]], axis=1).astype(jnp.bfloat16)
    reach = min(WINDOW // tok_rows, seq_count - 1)

    def advance(counter, state):
        current, current_seg, store, store_seg = state
        current, current_seg = from_behind((current, current_seg), "seq", 1)
        slot = reach - 1 - counter
        store = lax.dynamic_update_slice_in_dim(store, current[None], slot, 0)
        store_seg = lax.dynamic_update_slice_in_dim(store_seg, current_seg[None], slot, 0)
        return (current, current_seg, store, store_seg)

    store_init = jnp.zeros((reach, tok_rows, kv_cache.shape[1]), jnp.bfloat16)
    seg_init = jnp.zeros((reach, tok_rows), jnp.int32)
    final_state = lax.fori_loop(0, reach, advance, (kv_cache, seg_ids, store_init, seg_init))
    block_kv = jnp.concatenate(
        [final_state[2].reshape(reach * tok_rows, kv_cache.shape[1]), kv_cache], axis=0
    )
    block_seg = jnp.concatenate([final_state[3].reshape(reach * tok_rows), seg_ids], axis=0)
    key_index = (my_index - reach) * tok_rows + jnp.arange((reach + 1) * tok_rows, dtype=jnp.int32)
    live = (block_seg[None, :] == seg_ids[:, None]) & (key_index[None, :] <= token_index[:, None])
    live = live & (token_index[:, None] - key_index[None, :] < WINDOW) & (key_index[None, :] >= 0)
    all_keys = block_kv[:, :HD]
    all_values = block_kv[:, HD:]
    head_outputs = []
    for head_idx in range(local_heads):
        scores = lax.dot_general(
            queries[:, head_idx, :],
            all_keys,
            (((1,), (1,)), ((), ())),
            preferred_element_type=jnp.float32,
        ) * HD ** (-0.5)
        scores = jnp.where(live, scores, -1e30)
        peak = jnp.max(scores, axis=1, keepdims=True)
        powered = jnp.exp(scores - peak)
        weights = (powered / jnp.sum(powered, axis=1, keepdims=True)).astype(jnp.bfloat16)
        head_outputs.append(
            jnp.dot(weights, all_values, preferred_element_type=jnp.float32).astype(jnp.bfloat16)
        )
    attended = jnp.concatenate(head_outputs, axis=1)
    partial_value = jnp.dot(
        attended,
        lax.all_gather(w_out, "seq", axis=1, tiled=True),
        preferred_element_type=jnp.float32,
    )
    summed = lax.psum_scatter(
        partial_value.astype(jnp.bfloat16), "tp", scatter_dimension=1, tiled=True
    ).astype(jnp.float32)
    hidden = (tokens.astype(jnp.float32) + summed).astype(jnp.bfloat16)
    return (hidden, kv_cache)


def solution(mesh):
    in_specs = (P("seq", "tp"), P("seq"), P(), P("seq", "tp"), P("seq", None), P("tp", "seq"))
    out_specs = (P("seq", "tp"), P("seq", None))
    return jax.shard_map(
        per_device, mesh=mesh, in_specs=in_specs, out_specs=out_specs, check_vma=False
    )
```

profile of v0, /device:TPU:2, one launch (start us, length us, event | category | flops | bytes accessed | tf_op | source)
XLA Modules:
  0.0 562.5 jit_solution(2328956909194726290)
XLA Ops:
  10.2 18.5 %all_gather.12 = bf16[128,2560]{1,0:T(8,128)(2,1)S(1)} all-gather(bf16[128,640]{1,0:T(8,128)(2,1)} %param.8), channel_id=1, replica_groups=mesh['seq'=128,'tp'=4] {'tp'}, dimensions={1}, use_global_device_ids=true | all-gather | bytes 819200 | tf_op jit(solution)/shard_map/all_gather | solution.py:45
  28.9 31.9 %psum.7 = s32[32]{0:T(128)S(1)} all-reduce(s32[32]{0:T(128)S(1)} %convert_reduce_fusion), channel_id=1, replica_groups=mesh['seq'=128,'tp'=4] {'seq'}, use_global_device_ids=true, to_apply=%region_2.0 | all-reduce | flops 32 | bytes 256 | tf_op jit(solution)/shard_map/psum | solution.py:50
  62.4 85.6 %all-gather.7.cloned.1.call-done = bf16[128,20,512]{2,1,0:T(8,128)(2,1)} async-done(((bf16[1,20,512]{2,1,0:T(8,128)(2,1)}), bf16[128,20,512]{2,1,0:T(8,128)(2,1)}) %all-gather.7.cloned.1.call-update) | async-done | bytes 2621456 | tf_op jit(solution)/shard_map/all_gather | solution.py:61
  148.0 3.6 reshape.164
  154.9 125.2 %all-gather.9.cloned.1.call-done = bf16[128,20,512]{2,1,0:T(8,128)(2,1)} async-done(((bf16[1,20,512]{2,1,0:T(8,128)(2,1)}), bf16[128,20,512]{2,1,0:T(8,128)(2,1)}) %all-gather.9.cloned.1.call-update) | async-done | bytes 2621456 | tf_op jit(solution)/shard_map/all_gather | solution.py:56
  280.1 3.6 reshape.166
  287.7 223.8 %while.19 = (s32[]{:T(128)}, bf16[128,512]{1,0:T(8,128)(2,1)S(1)}, s32[128]{0:T(128)S(1)}, bf16[16,128,512]{2,1,0:T(8,128)(2,1)S(1)}, s32[16,128]{1,0:T(8,128)S(...) while((s32[]{:T(128)}, bf16[128,512]{1,0:T(8,128)(2,1)S(1)}, s32[128]{0:T(128)S(1)}, ...), condition=%wide.region_5.6_spmd, body=%wide.region_4.5_spmd.sunk | while | flops 6 | bytes 1052899 | solution.py:80
  287.7 2.3 collective-permute-start
  289.9 2.4 collective-permute-start.1
  292.3 9.4 %collective-permute-done.1 = s32[128]{0:T(128)S(1)} collective-permute-done((s32[128]{0:T(128)S(1)}, s32[128]{0:T(128)S(1)}, u32[]{:S(2)}, u32[]{:S(2)}) %collective-permute-start.1) | collective-permute-done | bytes 544 | tf_op jit(solution)/shard_map/while/body/eval_jaxpr/ppermute | solution.py:14
  303.8 1.9 collective-permute-start.1
  305.7 9.9 %collective-permute-done.1 = s32[128]{0:T(128)S(1)} collective-permute-done((s32[128]{0:T(128)S(1)}, s32[128]{0:T(128)S(1)}, u32[]{:S(2)}, u32[]{:S(2)}) %collective-permute-start.1) | collective-permute-done | bytes 544 | tf_op jit(solution)/shard_map/while/body/eval_jaxpr/ppermute | solution.py:14
  315.7 1.9 collective-permute-start
  317.6 1.9 collective-permute-start.1
  319.6 10.9 %collective-permute-done.1 = s32[128]{0:T(128)S(1)} collective-permute-done((s32[128]{0:T(128)S(1)}, s32[128]{0:T(128)S(1)}, u32[]{:S(2)}, u32[]{:S(2)}) %collective-permute-start.1) | collective-permute-done | bytes 544 | tf_op jit(solution)/shard_map/while/body/eval_jaxpr/ppermute | solution.py:14
  334.5 9.9 %collective-permute-done.1 = s32[128]{0:T(128)S(1)} collective-permute-done((s32[128]{0:T(128)S(1)}, s32[128]{0:T(128)S(1)}, u32[]{:S(2)}, u32[]{:S(2)}) %collective-permute-start.1) | collective-permute-done | bytes 544 | tf_op jit(solution)/shard_map/while/body/eval_jaxpr/ppermute | solution.py:14
  348.3 9.9 %collective-permute-done.1 = s32[128]{0:T(128)S(1)} collective-permute-done((s32[128]{0:T(128)S(1)}, s32[128]{0:T(128)S(1)}, u32[]{:S(2)}, u32[]{:S(2)}) %collective-permute-start.1) | collective-permute-done | bytes 544 | tf_op jit(solution)/shard_map/while/body/eval_jaxpr/ppermute | solution.py:14
  362.1 9.9 %collective-permute-done.1 = s32[128]{0:T(128)S(1)} collective-permute-done((s32[128]{0:T(128)S(1)}, s32[128]{0:T(128)S(1)}, u32[]{:S(2)}, u32[]{:S(2)}) %collective-permute-start.1) | collective-permute-done | bytes 544 | tf_op jit(solution)/shard_map/while/body/eval_jaxpr/ppermute | solution.py:14
  375.9 9.9 %collective-permute-done.1 = s32[128]{0:T(128)S(1)} collective-permute-done((s32[128]{0:T(128)S(1)}, s32[128]{0:T(128)S(1)}, u32[]{:S(2)}, u32[]{:S(2)}) %collective-permute-start.1) | collective-permute-done | bytes 544 | tf_op jit(solution)/shard_map/while/body/eval_jaxpr/ppermute | solution.py:14
  386.0 1.9 collective-permute-start
  387.9 1.9 collective-permute-start.1
  389.8 11.0 %collective-permute-done.1 = s32[128]{0:T(128)S(1)} collective-permute-done((s32[128]{0:T(128)S(1)}, s32[128]{0:T(128)S(1)}, u32[]{:S(2)}, u32[]{:S(2)}) %collective-permute-start.1) | collective-permute-done | bytes 544 | tf_op jit(solution)/shard_map/while/body/eval_jaxpr/ppermute | solution.py:14
  404.8 9.9 %collective-permute-done.1 = s32[128]{0:T(128)S(1)} collective-permute-done((s32[128]{0:T(128)S(1)}, s32[128]{0:T(128)S(1)}, u32[]{:S(2)}, u32[]{:S(2)}) %collective-permute-start.1) | collective-permute-done | bytes 544 | tf_op jit(solution)/shard_map/while/body/eval_jaxpr/ppermute | solution.py:14
  418.6 9.9 %collective-permute-done.1 = s32[128]{0:T(128)S(1)} collective-permute-done((s32[128]{0:T(128)S(1)}, s32[128]{0:T(128)S(1)}, u32[]{:S(2)}, u32[]{:S(2)}) %collective-permute-start.1) | collective-permute-done | bytes 544 | tf_op jit(solution)/shard_map/while/body/eval_jaxpr/ppermute | solution.py:14
  432.4 9.9 %collective-permute-done.1 = s32[128]{0:T(128)S(1)} collective-permute-done((s32[128]{0:T(128)S(1)}, s32[128]{0:T(128)S(1)}, u32[]{:S(2)}, u32[]{:S(2)}) %collective-permute-start.1) | collective-permute-done | bytes 544 | tf_op jit(solution)/shard_map/while/body/eval_jaxpr/ppermute | solution.py:14
  446.2 9.9 %collective-permute-done.1 = s32[128]{0:T(128)S(1)} collective-permute-done((s32[128]{0:T(128)S(1)}, s32[128]{0:T(128)S(1)}, u32[]{:S(2)}, u32[]{:S(2)}) %collective-permute-start.1) | collective-permute-done | bytes 544 | tf_op jit(solution)/shard_map/while/body/eval_jaxpr/ppermute | solution.py:14
  460.1 9.9 %collective-permute-done.1 = s32[128]{0:T(128)S(1)} collective-permute-done((s32[128]{0:T(128)S(1)}, s32[128]{0:T(128)S(1)}, u32[]{:S(2)}, u32[]{:S(2)}) %collective-permute-start.1) | collective-permute-done | bytes 544 | tf_op jit(solution)/shard_map/while/body/eval_jaxpr/ppermute | solution.py:14
  473.9 9.9 %collective-permute-done.1 = s32[128]{0:T(128)S(1)} collective-permute-done((s32[128]{0:T(128)S(1)}, s32[128]{0:T(128)S(1)}, u32[]{:S(2)}, u32[]{:S(2)}) %collective-permute-start.1) | collective-permute-done | bytes 544 | tf_op jit(solution)/shard_map/while/body/eval_jaxpr/ppermute | solution.py:14
  487.7 9.9 %collective-permute-done.1 = s32[128]{0:T(128)S(1)} collective-permute-done((s32[128]{0:T(128)S(1)}, s32[128]{0:T(128)S(1)}, u32[]{:S(2)}, u32[]{:S(2)}) %collective-permute-start.1) | collective-permute-done | bytes 544 | tf_op jit(solution)/shard_map/while/body/eval_jaxpr/ppermute | solution.py:14
  501.5 9.9 %collective-permute-done.1 = s32[128]{0:T(128)S(1)} collective-permute-done((s32[128]{0:T(128)S(1)}, s32[128]{0:T(128)S(1)}, u32[]{:S(2)}, u32[]{:S(2)}) %collective-permute-start.1) | collective-permute-done | bytes 544 | tf_op jit(solution)/shard_map/while/body/eval_jaxpr/ppermute | solution.py:14
  515.1 3.6 reshape.168
  520.9 33.3 %reduce-scatter.4.cloned.1.call-done = bf16[640,128]{1,0:T(8,128)(2,1)} async-done(((bf16[2560,128]{1,0:T(8,128)(2,1)}), bf16[640,128]{1,0:T(8,128)(2,1)}) %reduce-scatter.4.cloned.1.call-update) | async-done | bytes 163856
  (173 shorter events, 68.2 us)
Async XLA Ops:
  7.2 140.8 %all-gather.7.cloned.1.call-start = ((), (), s32[]{:S(2)}) async-start(), calls=%async_computation.1 | async-start | bytes 3170304 | tf_op jit(solution)/shard_map/all_gather | solution.py:61
  7.9 272.1 %all-gather.9.cloned.1.call-start = ((), (), s32[]{:S(2)}) async-start(), calls=%async_computation.2 | async-start | bytes 3170304 | tf_op jit(solution)/shard_map/all_gather | solution.py:56
  8.7 506.4 %all-gather.11.cloned.1.call-start = ((), (), s32[]{:S(2)}) async-start(), calls=%async_computation.3 | async-start | bytes 3170304 | tf_op jit(solution)/shard_map/all_gather | solution.py:108
  9.4 544.8 %reduce-scatter.4.cloned.1.call-start = ((), (), s32[]{:S(2)}) async-start(), calls=%async_computation.4 | async-start | bytes 819200
  287.7 14.1 %collective-permute-start = (bf16[128,512]{1,0:T(8,128)(2,1)S(1)}, bf16[128,512]{1,0:T(8,128)(2,1)S(1)}, u32[]{:S(2)}, u32[]{:S(2)}) collective-permute-start(bf16[128,512]{1,0:T(8,128)(2,1)S(1)} %get-tuple-element.171), channel_id=1, source_target_pairs={{0,4},{4,8},{8,12},{12,16},{16,20},{20,24},{24,28},{28,32},{32,36}... | collective-permute-start | bytes 393224 | tf_op jit(solution)/shard_map/while/body/eval_jaxpr/ppermute | solution.py:14
  289.9 11.8 %collective-permute-start.1 = (s32[128]{0:T(128)S(1)}, s32[128]{0:T(128)S(1)}, u32[]{:S(2)}, u32[]{:S(2)}) collective-permute-start(s32[128]{0:T(128)S(1)} %get-tuple-element.172), channel_id=1, source_target_pairs={{0,4},{4,8},{8,12},{12,16},{16,20},{20,24},{24,28},{28,32},{32,36}... | collective-permute-start | bytes 1544 | tf_op jit(solution)/shard_map/while/body/eval_jaxpr/ppermute | solution.py:14
  301.8 13.8 %collective-permute-start = (bf16[128,512]{1,0:T(8,128)(2,1)S(1)}, bf16[128,512]{1,0:T(8,128)(2,1)S(1)}, u32[]{:S(2)}, u32[]{:S(2)}) collective-permute-start(bf16[128,512]{1,0:T(8,128)(2,1)S(1)} %get-tuple-element.171), channel_id=1, source_target_pairs={{0,4},{4,8},{8,12},{12,16},{16,20},{20,24},{24,28},{28,32},{32,36}... | collective-permute-start | bytes 393224 | tf_op jit(solution)/shard_map/while/body/eval_jaxpr/ppermute | solution.py:14
  303.8 11.9 %collective-permute-start.1 = (s32[128]{0:T(128)S(1)}, s32[128]{0:T(128)S(1)}, u32[]{:S(2)}, u32[]{:S(2)}) collective-permute-start(s32[128]{0:T(128)S(1)} %get-tuple-element.172), channel_id=1, source_target_pairs={{0,4},{4,8},{8,12},{12,16},{16,20},{20,24},{24,28},{28,32},{32,36}... | collective-permute-start | bytes 1544 | tf_op jit(solution)/shard_map/while/body/eval_jaxpr/ppermute | solution.py:14
  315.7 14.8 %collective-permute-start = (bf16[128,512]{1,0:T(8,128)(2,1)S(1)}, bf16[128,512]{1,0:T(8,128)(2,1)S(1)}, u32[]{:S(2)}, u32[]{:S(2)}) collective-permute-start(bf16[128,512]{1,0:T(8,128)(2,1)S(1)} %get-tuple-element.171), channel_id=1, source_target_pairs={{0,4},{4,8},{8,12},{12,16},{16,20},{20,24},{24,28},{28,32},{32,36}... | collective-permute-start | bytes 393224 | tf_op jit(solution)/shard_map/while/body/eval_jaxpr/ppermute | solution.py:14
  317.6 12.9 %collective-permute-start.1 = (s32[128]{0:T(128)S(1)}, s32[128]{0:T(128)S(1)}, u32[]{:S(2)}, u32[]{:S(2)}) collective-permute-start(s32[128]{0:T(128)S(1)} %get-tuple-element.172), channel_id=1, source_target_pairs={{0,4},{4,8},{8,12},{12,16},{16,20},{20,24},{24,28},{28,32},{32,36}... | collective-permute-start | bytes 1544 | tf_op jit(solution)/shard_map/while/body/eval_jaxpr/ppermute | solution.py:14
  330.6 13.8 %collective-permute-start = (bf16[128,512]{1,0:T(8,128)(2,1)S(1)}, bf16[128,512]{1,0:T(8,128)(2,1)S(1)}, u32[]{:S(2)}, u32[]{:S(2)}) collective-permute-start(bf16[128,512]{1,0:T(8,128)(2,1)S(1)} %get-tuple-element.171), channel_id=1, source_target_pairs={{0,4},{4,8},{8,12},{12,16},{16,20},{20,24},{24,28},{28,32},{32,36}... | collective-permute-start | bytes 393224 | tf_op jit(solution)/shard_map/while/body/eval_jaxpr/ppermute | solution.py:14
  332.5 11.8 %collective-permute-start.1 = (s32[128]{0:T(128)S(1)}, s32[128]{0:T(128)S(1)}, u32[]{:S(2)}, u32[]{:S(2)}) collective-permute-start(s32[128]{0:T(128)S(1)} %get-tuple-element.172), channel_id=1, source_target_pairs={{0,4},{4,8},{8,12},{12,16},{16,20},{20,24},{24,28},{28,32},{32,36}... | collective-permute-start | bytes 1544 | tf_op jit(solution)/shard_map/while/body/eval_jaxpr/ppermute | solution.py:14
  344.4 13.8 %collective-permute-start = (bf16[128,512]{1,0:T(8,128)(2,1)S(1)}, bf16[128,512]{1,0:T(8,128)(2,1)S(1)}, u32[]{:S(2)}, u32[]{:S(2)}) collective-permute-start(bf16[128,512]{1,0:T(8,128)(2,1)S(1)} %get-tuple-element.171), channel_id=1, source_target_pairs={{0,4},{4,8},{8,12},{12,16},{16,20},{20,24},{24,28},{28,32},{32,36}... | collective-permute-start | bytes 393224 | tf_op jit(solution)/shard_map/while/body/eval_jaxpr/ppermute | solution.py:14
  346.4 11.8 %collective-permute-start.1 = (s32[128]{0:T(128)S(1)}, s32[128]{0:T(128)S(1)}, u32[]{:S(2)}, u32[]{:S(2)}) collective-permute-start(s32[128]{0:T(128)S(1)} %get-tuple-element.172), channel_id=1, source_target_pairs={{0,4},{4,8},{8,12},{12,16},{16,20},{20,24},{24,28},{28,32},{32,36}... | collective-permute-start | bytes 1544 | tf_op jit(solution)/shard_map/while/body/eval_jaxpr/ppermute | solution.py:14
  358.3 13.8 %collective-permute-start = (bf16[128,512]{1,0:T(8,128)(2,1)S(1)}, bf16[128,512]{1,0:T(8,128)(2,1)S(1)}, u32[]{:S(2)}, u32[]{:S(2)}) collective-permute-start(bf16[128,512]{1,0:T(8,128)(2,1)S(1)} %get-tuple-element.171), channel_id=1, source_target_pairs={{0,4},{4,8},{8,12},{12,16},{16,20},{20,24},{24,28},{28,32},{32,36}... | collective-permute-start | bytes 393224 | tf_op jit(solution)/shard_map/while/body/eval_jaxpr/ppermute | solution.py:14
  360.2 11.8 %collective-permute-start.1 = (s32[128]{0:T(128)S(1)}, s32[128]{0:T(128)S(1)}, u32[]{:S(2)}, u32[]{:S(2)}) collective-permute-start(s32[128]{0:T(128)S(1)} %get-tuple-element.172), channel_id=1, source_target_pairs={{0,4},{4,8},{8,12},{12,16},{16,20},{20,24},{24,28},{28,32},{32,36}... | collective-permute-start | bytes 1544 | tf_op jit(solution)/shard_map/while/body/eval_jaxpr/ppermute | solution.py:14
  372.1 13.8 %collective-permute-start = (bf16[128,512]{1,0:T(8,128)(2,1)S(1)}, bf16[128,512]{1,0:T(8,128)(2,1)S(1)}, u32[]{:S(2)}, u32[]{:S(2)}) collective-permute-start(bf16[128,512]{1,0:T(8,128)(2,1)S(1)} %get-tuple-element.171), channel_id=1, source_target_pairs={{0,4},{4,8},{8,12},{12,16},{16,20},{20,24},{24,28},{28,32},{32,36}... | collective-permute-start | bytes 393224 | tf_op jit(solution)/shard_map/while/body/eval_jaxpr/ppermute | solution.py:14
  374.0 11.9 %collective-permute-start.1 = (s32[128]{0:T(128)S(1)}, s32[128]{0:T(128)S(1)}, u32[]{:S(2)}, u32[]{:S(2)}) collective-permute-start(s32[128]{0:T(128)S(1)} %get-tuple-element.172), channel_id=1, source_target_pairs={{0,4},{4,8},{8,12},{12,16},{16,20},{20,24},{24,28},{28,32},{32,36}... | collective-permute-start | bytes 1544 | tf_op jit(solution)/shard_map/while/body/eval_jaxpr/ppermute | solution.py:14
  386.0 14.9 %collective-permute-start = (bf16[128,512]{1,0:T(8,128)(2,1)S(1)}, bf16[128,512]{1,0:T(8,128)(2,1)S(1)}, u32[]{:S(2)}, u32[]{:S(2)}) collective-permute-start(bf16[128,512]{1,0:T(8,128)(2,1)S(1)} %get-tuple-element.171), channel_id=1, source_target_pairs={{0,4},{4,8},{8,12},{12,16},{16,20},{20,24},{24,28},{28,32},{32,36}... | collective-permute-start | bytes 393224 | tf_op jit(solution)/shard_map/while/body/eval_jaxpr/ppermute | solution.py:14
  387.9 12.9 %collective-permute-start.1 = (s32[128]{0:T(128)S(1)}, s32[128]{0:T(128)S(1)}, u32[]{:S(2)}, u32[]{:S(2)}) collective-permute-start(s32[128]{0:T(128)S(1)} %get-tuple-element.172), channel_id=1, source_target_pairs={{0,4},{4,8},{8,12},{12,16},{16,20},{20,24},{24,28},{28,32},{32,36}... | collective-permute-start | bytes 1544 | tf_op jit(solution)/shard_map/while/body/eval_jaxpr/ppermute | solution.py:14
  400.9 13.8 %collective-permute-start = (bf16[128,512]{1,0:T(8,128)(2,1)S(1)}, bf16[128,512]{1,0:T(8,128)(2,1)S(1)}, u32[]{:S(2)}, u32[]{:S(2)}) collective-permute-start(bf16[128,512]{1,0:T(8,128)(2,1)S(1)} %get-tuple-element.171), channel_id=1, source_target_pairs={{0,4},{4,8},{8,12},{12,16},{16,20},{20,24},{24,28},{28,32},{32,36}... | collective-permute-start | bytes 393224 | tf_op jit(solution)/shard_map/while/body/eval_jaxpr/ppermute | solution.py:14
  402.8 11.8 %collective-permute-start.1 = (s32[128]{0:T(128)S(1)}, s32[128]{0:T(128)S(1)}, u32[]{:S(2)}, u32[]{:S(2)}) collective-permute-start(s32[128]{0:T(128)S(1)} %get-tuple-element.172), channel_id=1, source_target_pairs={{0,4},{4,8},{8,12},{12,16},{16,20},{20,24},{24,28},{28,32},{32,36}... | collective-permute-start | bytes 1544 | tf_op jit(solution)/shard_map/while/body/eval_jaxpr/ppermute | solution.py:14
  414.7 13.8 %collective-permute-start = (bf16[128,512]{1,0:T(8,128)(2,1)S(1)}, bf16[128,512]{1,0:T(8,128)(2,1)S(1)}, u32[]{:S(2)}, u32[]{:S(2)}) collective-permute-start(bf16[128,512]{1,0:T(8,128)(2,1)S(1)} %get-tuple-element.171), channel_id=1, source_target_pairs={{0,4},{4,8},{8,12},{12,16},{16,20},{20,24},{24,28},{28,32},{32,36}... | collective-permute-start | bytes 393224 | tf_op jit(solution)/shard_map/while/body/eval_jaxpr/ppermute | solution.py:14
  416.7 11.8 %collective-permute-start.1 = (s32[128]{0:T(128)S(1)}, s32[128]{0:T(128)S(1)}, u32[]{:S(2)}, u32[]{:S(2)}) collective-permute-start(s32[128]{0:T(128)S(1)} %get-tuple-element.172), channel_id=1, source_target_pairs={{0,4},{4,8},{8,12},{12,16},{16,20},{20,24},{24,28},{28,32},{32,36}... | collective-permute-start | bytes 1544 | tf_op jit(solution)/shard_map/while/body/eval_jaxpr/ppermute | solution.py:14
  428.6 13.8 %collective-permute-start = (bf16[128,512]{1,0:T(8,128)(2,1)S(1)}, bf16[128,512]{1,0:T(8,128)(2,1)S(1)}, u32[]{:S(2)}, u32[]{:S(2)}) collective-permute-start(bf16[128,512]{1,0:T(8,128)(2,1)S(1)} %get-tuple-element.171), channel_id=1, source_target_pairs={{0,4},{4,8},{8,12},{12,16},{16,20},{20,24},{24,28},{28,32},{32,36}... | collective-permute-start | bytes 393224 | tf_op jit(solution)/shard_map/while/body/eval_jaxpr/ppermute | solution.py:14
  430.5 11.8 %collective-permute-start.1 = (s32[128]{0:T(128)S(1)}, s32[128]{0:T(128)S(1)}, u32[]{:S(2)}, u32[]{:S(2)}) collective-permute-start(s32[128]{0:T(128)S(1)} %get-tuple-element.172), channel_id=1, source_target_pairs={{0,4},{4,8},{8,12},{12,16},{16,20},{20,24},{24,28},{28,32},{32,36}... | collective-permute-start | bytes 1544 | tf_op jit(solution)/shard_map/while/body/eval_jaxpr/ppermute | solution.py:14
  442.4 13.8 %collective-permute-start = (bf16[128,512]{1,0:T(8,128)(2,1)S(1)}, bf16[128,512]{1,0:T(8,128)(2,1)S(1)}, u32[]{:S(2)}, u32[]{:S(2)}) collective-permute-start(bf16[128,512]{1,0:T(8,128)(2,1)S(1)} %get-tuple-element.171), channel_id=1, source_target_pairs={{0,4},{4,8},{8,12},{12,16},{16,20},{20,24},{24,28},{28,32},{32,36}... | collective-permute-start | bytes 393224 | tf_op jit(solution)/shard_map/while/body/eval_jaxpr/ppermute | solution.py:14
  456.2 13.8 %collective-permute-start = (bf16[128,512]{1,0:T(8,128)(2,1)S(1)}, bf16[128,512]{1,0:T(8,128)(2,1)S(1)}, u32[]{:S(2)}, u32[]{:S(2)}) collective-permute-start(bf16[128,512]{1,0:T(8,128)(2,1)S(1)} %get-tuple-element.171), channel_id=1, source_target_pairs={{0,4},{4,8},{8,12},{12,16},{16,20},{20,24},{24,28},{28,32},{32,36}... | collective-permute-start | bytes 393224 | tf_op jit(solution)/shard_map/while/body/eval_jaxpr/ppermute | solution.py:14
  470.0 13.8 %collective-permute-start = (bf16[128,512]{1,0:T(8,128)(2,1)S(1)}, bf16[128,512]{1,0:T(8,128)(2,1)S(1)}, u32[]{:S(2)}, u32[]{:S(2)}) collective-permute-start(bf16[128,512]{1,0:T(8,128)(2,1)S(1)} %get-tuple-element.171), channel_id=1, source_target_pairs={{0,4},{4,8},{8,12},{12,16},{16,20},{20,24},{24,28},{28,32},{32,36}... | collective-permute-start | bytes 393224 | tf_op jit(solution)/shard_map/while/body/eval_jaxpr/ppermute | solution.py:14
  483.9 13.8 %collective-permute-start = (bf16[128,512]{1,0:T(8,128)(2,1)S(1)}, bf16[128,512]{1,0:T(8,128)(2,1)S(1)}, u32[]{:S(2)}, u32[]{:S(2)}) collective-permute-start(bf16[128,512]{1,0:T(8,128)(2,1)S(1)} %get-tuple-element.171), channel_id=1, source_target_pairs={{0,4},{4,8},{8,12},{12,16},{16,20},{20,24},{24,28},{28,32},{32,36}... | collective-permute-start | bytes 393224 | tf_op jit(solution)/shard_map/while/body/eval_jaxpr/ppermute | solution.py:14
  485.8 11.8 %collective-permute-start.1 = (s32[128]{0:T(128)S(1)}, s32[128]{0:T(128)S(1)}, u32[]{:S(2)}, u32[]{:S(2)}) collective-permute-start(s32[128]{0:T(128)S(1)} %get-tuple-element.172), channel_id=1, source_target_pairs={{0,4},{4,8},{8,12},{12,16},{16,20},{20,24},{24,28},{28,32},{32,36}... | collective-permute-start | bytes 1544 | tf_op jit(solution)/shard_map/while/body/eval_jaxpr/ppermute | solution.py:14
  497.7 13.8 %collective-permute-start = (bf16[128,512]{1,0:T(8,128)(2,1)S(1)}, bf16[128,512]{1,0:T(8,128)(2,1)S(1)}, u32[]{:S(2)}, u32[]{:S(2)}) collective-permute-start(bf16[128,512]{1,0:T(8,128)(2,1)S(1)} %get-tuple-element.171), channel_id=1, source_target_pairs={{0,4},{4,8},{8,12},{12,16},{16,20},{20,24},{24,28},{28,32},{32,36}... | collective-permute-start | bytes 393224 | tf_op jit(solution)/shard_map/while/body/eval_jaxpr/ppermute | solution.py:14
  (14 other events, 1181.9 us)
Sparse Core Ops, SparseCore 0:
  12.7 135.2 all-gather.6
  152.7 127.3 all-gather.8
  284.8 126.9 all-gather.10
  521.0 33.1 reduce-scatter.3
where the time goes:
time: 564 us; the launch traced here: 562 us
  waiting for transfers between devices  406 us (72%)
  starting transfers between devices  62.4 us (11%)
  blocking collectives  50.3 us (9%)
  local copies, waits for them, and re-layouts  16.6 us (3%)
  between operations  14.1 us (2%)
  other arithmetic  6.51 us (1%)
  matrix products  5.67 us (1%)
    ppermute x32, waiting for transfers between devices, from_behind(): return lax.ppermute(x, axis, pairs)  160 us
    all_gather x1, waiting for transfers between devices, per_device(): lax.all_gather(w_query, 'seq', axis=0, tiled=True)  125 us
    all_gather x1, waiting for transfers between devices, per_device(): lax.all_gather(w_keyval, 'seq', axis=0, tiled=True)  85.6 us
    ppermute x32, starting transfers between devices, from_behind(): return lax.ppermute(x, axis, pairs)  62.3 us
    unnamed x5, waiting for transfers between devices  35.4 us
    psum x1, blocking collectives, per_device(): starts = lax.psum(below, 'seq')  31.9 us
    all_gather x1, blocking collectives, per_device(): gathered = lax.all_gather(tokens, 'tp', axis=1, tiled=True)  18.5 us
    unnamed x27, local copies, waits for them, and re-layouts  13.8 us
  transfers between devices with their start and end apart: 36, of which 19 were waited for; matrix products, arithmetic and copies ran while one was open for 4% of the time, Pallas kernels for 0%

commit v1 on v0

--- a/solution.py
+++ b/solution.py
@@ -47,7 +47,7 @@
     seg_total = tok_rows * seq_count // SEG_MEAN
     labels = jnp.arange(seg_total, dtype=jnp.int32)
     below = jnp.sum((seg_ids[None, :] < labels[:, None]).astype(jnp.int32), axis=1)
-    starts = lax.psum(below, "seq")
+    starts = jax.lax.all_gather(below, "seq").sum(axis=0)
     own_start = jnp.sum(jnp.where(seg_ids[:, None] == labels[None, :], starts[None, :], 0), axis=1)
     token_index = my_index * tok_rows + jnp.arange(tok_rows, dtype=jnp.int32)
     positions = (token_index - own_start).astype(jnp.float32)

time: 564 us -> 1060 us (1.88)
  blocking collectives: 50.3 us -> 755 us
  waiting for transfers between devices: 406 us -> 193 us
    unnamed x0 -> x1, blocking collectives: none -> 737 us
    all_gather x1, waiting for transfers between devices: 125 us -> 0.01 us  [per_device(): lax.all_gather(w_query, 'seq', axis=0, tiled=True)]
    all_gather x1, waiting for transfers between devices: 85.6 us -> 0.01 us  [per_device(): lax.all_gather(w_keyval, 'seq', axis=0, tiled=True)]
    psum x1 -> x0, blocking collectives: 31.9 us -> none  [per_device(): starts = lax.psum(below, 'seq')]
  transfers between devices with their start and end apart: 36 -> 36, of which waited for: 19 -> 17; matrix products, arithmetic and copies ran while one was open for 4% -> 2% of each run, Pallas kernels for 0% -> 0%
where the time goes in v1:
time: 1060 us
  blocking collectives  755 us (71%)
  waiting for transfers between devices  193 us (18%)
  starting transfers between devices  61.7 us (6%)
  local copies, waits for them, and re-layouts  18.3 us (2%)
  between operations  14.7 us (1%)
    unnamed x1, blocking collectives  737 us
    ppermute x32, waiting for transfers between devices, from_behind(): return lax.ppermute(x, axis, pairs)  159 us
    ppermute x32, starting transfers between devices, from_behind(): return lax.ppermute(x, axis, pairs)  61.6 us
    unnamed x5, waiting for transfers between devices  33.9 us
  transfers between devices with their start and end apart: 36, of which 17 were waited for; matrix products, arithmetic and copies ran while one was open for 2% of the time, Pallas kernels for 0%

profile of v1, /device:TPU:2, one launch (start us, length us, event | category | flops | bytes accessed | tf_op | source)
XLA Modules:
  0.0 1055.9 jit_solution(931985239734382381)
XLA Ops:
  10.2 18.5 %all_gather.18 = bf16[128,2560]{1,0:T(8,128)(2,1)S(1)} all-gather(bf16[128,640]{1,0:T(8,128)(2,1)} %param.8), channel_id=1, replica_groups=mesh['seq'=128,'tp'=4] {'tp'}, dimensions={1}, use_global_device_ids=true | all-gather | bytes 819200 | tf_op jit(solution)/shard_map/all_gather | solution.py:45
  31.2 736.5 %all-reduce = s32[4096]{0:T(1024)S(1)} all-reduce(s32[4096]{0:T(1024)S(1)} %dynamic-update-slice), channel_id=2, replica_groups=mesh['seq'=128,'tp'=4] {'seq'}, use_global_device_ids=true, to_apply=%add | all-reduce | flops 4096 | bytes 32768
  769.5 3.6 reshape.168
  776.4 3.6 reshape.170
  784.0 222.3 %while.19 = (s32[]{:T(128)}, bf16[128,512]{1,0:T(8,128)(2,1)S(1)}, s32[128]{0:T(128)S(1)}, bf16[16,128,512]{2,1,0:T(8,128)(2,1)S(1)}, s32[16,128]{1,0:T(8,128)S(...) while((s32[]{:T(128)}, bf16[128,512]{1,0:T(8,128)(2,1)S(1)}, s32[128]{0:T(128)S(1)}, ...), condition=%wide.region_5.6_spmd, body=%wide.region_4.5_spmd.sunk | while | flops 6 | bytes 1052899 | solution.py:80
  784.0 2.0 collective-permute-start
  786.0 1.9 collective-permute-start.1
  787.9 9.9 collective-permute-done.1
  801.8 9.9 collective-permute-done.1
  811.7 1.9 collective-permute-start
  813.7 1.9 collective-permute-start.1
  815.6 9.9 collective-permute-done.1
  829.4 9.9 collective-permute-done.1
  839.4 1.9 collective-permute-start
  843.2 9.9 collective-permute-done.1
  857.1 9.9 collective-permute-done.1
  870.9 9.9 collective-permute-done.1
  884.8 10.8 %collective-permute-done.1 = s32[128]{0:T(128)S(1)} collective-permute-done((s32[128]{0:T(128)S(1)}, s32[128]{0:T(128)S(1)}, u32[]{:S(2)}, u32[]{:S(2)}) %collective-permute-start.1) | collective-permute-done | bytes 544 | tf_op jit(solution)/shard_map/while/body/eval_jaxpr/ppermute | solution.py:14
  895.7 1.9 collective-permute-start
  897.6 1.9 collective-permute-start.1
  899.6 9.9 collective-permute-done.1
  913.4 9.9 collective-permute-done.1
  923.3 1.9 collective-permute-start
  925.3 1.9 collective-permute-start.1
  927.2 9.9 collective-permute-done.1
  941.0 9.9 collective-permute-done.1
  954.9 9.9 collective-permute-done.1
  968.7 9.9 collective-permute-done.1
  982.5 9.9 collective-permute-done.1
  996.3 9.9 collective-permute-done.1
  1010.0 3.6 reshape.172
  1015.7 31.8 %reduce-scatter.4.cloned.1.call-done = bf16[640,128]{1,0:T(8,128)(2,1)} async-done(((bf16[2560,128]{1,0:T(8,128)(2,1)}), bf16[640,128]{1,0:T(8,128)(2,1)}) %reduce-scatter.4.cloned.1.call-update) | async-done | bytes 163856
  (178 shorter events, 66.2 us)
Async XLA Ops:
  7.2 762.3 %all-gather.8.cloned.1.call-start = ((), (), s32[]{:S(2)}) async-start(), calls=%async_computation.1 | async-start | bytes 3170304 | tf_op jit(solution)/shard_map/all_gather | solution.py:61
  7.9 768.5 %all-gather.10.cloned.1.call-start = ((), (), s32[]{:S(2)}) async-start(), calls=%async_computation.2 | async-start | bytes 3170304 | tf_op jit(solution)/shard_map/all_gather | solution.py:56
  8.7 1001.3 %all-gather.12.cloned.1.call-start = ((), (), s32[]{:S(2)}) async-start(), calls=%async_computation.3 | async-start | bytes 3170304 | tf_op jit(solution)/shard_map/all_gather | solution.py:108
  9.4 1038.1 %reduce-scatter.4.cloned.1.call-start = ((), (), s32[]{:S(2)}) async-start(), calls=%async_computation.4 | async-start | bytes 819200
  784.0 13.9 %collective-permute-start = (bf16[128,512]{1,0:T(8,128)(2,1)S(1)}, bf16[128,512]{1,0:T(8,128)(2,1)S(1)}, u32[]{:S(2)}, u32[]{:S(2)}) collective-permute-start(bf16[128,512]{1,0:T(8,128)(2,1)S(1)} %get-tuple-element.171), channel_id=1, source_target_pairs={{0,4},{4,8},{8,12},{12,16},{16,20},{20,24},{24,28},{28,32},{32,36}... | collective-permute-start | bytes 393224 | tf_op jit(solution)/shard_map/while/body/eval_jaxpr/ppermute | solution.py:14
  786.0 11.8 %collective-permute-start.1 = (s32[128]{0:T(128)S(1)}, s32[128]{0:T(128)S(1)}, u32[]{:S(2)}, u32[]{:S(2)}) collective-permute-start(s32[128]{0:T(128)S(1)} %get-tuple-element.172), channel_id=1, source_target_pairs={{0,4},{4,8},{8,12},{12,16},{16,20},{20,24},{24,28},{28,32},{32,36}... | collective-permute-start | bytes 1544 | tf_op jit(solution)/shard_map/while/body/eval_jaxpr/ppermute | solution.py:14
  797.9 13.8 %collective-permute-start = (bf16[128,512]{1,0:T(8,128)(2,1)S(1)}, bf16[128,512]{1,0:T(8,128)(2,1)S(1)}, u32[]{:S(2)}, u32[]{:S(2)}) collective-permute-start(bf16[128,512]{1,0:T(8,128)(2,1)S(1)} %get-tuple-element.171), channel_id=1, source_target_pairs={{0,4},{4,8},{8,12},{12,16},{16,20},{20,24},{24,28},{28,32},{32,36}... | collective-permute-start | bytes 393224 | tf_op jit(solution)/shard_map/while/body/eval_jaxpr/ppermute | solution.py:14
  799.8 11.8 %collective-permute-start.1 = (s32[128]{0:T(128)S(1)}, s32[128]{0:T(128)S(1)}, u32[]{:S(2)}, u32[]{:S(2)}) collective-permute-start(s32[128]{0:T(128)S(1)} %get-tuple-element.172), channel_id=1, source_target_pairs={{0,4},{4,8},{8,12},{12,16},{16,20},{20,24},{24,28},{28,32},{32,36}... | collective-permute-start | bytes 1544 | tf_op jit(solution)/shard_map/while/body/eval_jaxpr/ppermute | solution.py:14
  811.7 13.8 %collective-permute-start = (bf16[128,512]{1,0:T(8,128)(2,1)S(1)}, bf16[128,512]{1,0:T(8,128)(2,1)S(1)}, u32[]{:S(2)}, u32[]{:S(2)}) collective-permute-start(bf16[128,512]{1,0:T(8,128)(2,1)S(1)} %get-tuple-element.171), channel_id=1, source_target_pairs={{0,4},{4,8},{8,12},{12,16},{16,20},{20,24},{24,28},{28,32},{32,36}... | collective-permute-start | bytes 393224 | tf_op jit(solution)/shard_map/while/body/eval_jaxpr/ppermute | solution.py:14
  813.7 11.8 %collective-permute-start.1 = (s32[128]{0:T(128)S(1)}, s32[128]{0:T(128)S(1)}, u32[]{:S(2)}, u32[]{:S(2)}) collective-permute-start(s32[128]{0:T(128)S(1)} %get-tuple-element.172), channel_id=1, source_target_pairs={{0,4},{4,8},{8,12},{12,16},{16,20},{20,24},{24,28},{28,32},{32,36}... | collective-permute-start | bytes 1544 | tf_op jit(solution)/shard_map/while/body/eval_jaxpr/ppermute | solution.py:14
  825.6 13.8 %collective-permute-start = (bf16[128,512]{1,0:T(8,128)(2,1)S(1)}, bf16[128,512]{1,0:T(8,128)(2,1)S(1)}, u32[]{:S(2)}, u32[]{:S(2)}) collective-permute-start(bf16[128,512]{1,0:T(8,128)(2,1)S(1)} %get-tuple-element.171), channel_id=1, source_target_pairs={{0,4},{4,8},{8,12},{12,16},{16,20},{20,24},{24,28},{28,32},{32,36}... | collective-permute-start | bytes 393224 | tf_op jit(solution)/shard_map/while/body/eval_jaxpr/ppermute | solution.py:14
  827.5 11.8 %collective-permute-start.1 = (s32[128]{0:T(128)S(1)}, s32[128]{0:T(128)S(1)}, u32[]{:S(2)}, u32[]{:S(2)}) collective-permute-start(s32[128]{0:T(128)S(1)} %get-tuple-element.172), channel_id=1, source_target_pairs={{0,4},{4,8},{8,12},{12,16},{16,20},{20,24},{24,28},{28,32},{32,36}... | collective-permute-start | bytes 1544 | tf_op jit(solution)/shard_map/while/body/eval_jaxpr/ppermute | solution.py:14
  839.4 13.8 %collective-permute-start = (bf16[128,512]{1,0:T(8,128)(2,1)S(1)}, bf16[128,512]{1,0:T(8,128)(2,1)S(1)}, u32[]{:S(2)}, u32[]{:S(2)}) collective-permute-start(bf16[128,512]{1,0:T(8,128)(2,1)S(1)} %get-tuple-element.171), channel_id=1, source_target_pairs={{0,4},{4,8},{8,12},{12,16},{16,20},{20,24},{24,28},{28,32},{32,36}... | collective-permute-start | bytes 393224 | tf_op jit(solution)/shard_map/while/body/eval_jaxpr/ppermute | solution.py:14
  841.3 11.8 %collective-permute-start.1 = (s32[128]{0:T(128)S(1)}, s32[128]{0:T(128)S(1)}, u32[]{:S(2)}, u32[]{:S(2)}) collective-permute-start(s32[128]{0:T(128)S(1)} %get-tuple-element.172), channel_id=1, source_target_pairs={{0,4},{4,8},{8,12},{12,16},{16,20},{20,24},{24,28},{28,32},{32,36}... | collective-permute-start | bytes 1544 | tf_op jit(solution)/shard_map/while/body/eval_jaxpr/ppermute | solution.py:14
  853.2 13.8 %collective-permute-start = (bf16[128,512]{1,0:T(8,128)(2,1)S(1)}, bf16[128,512]{1,0:T(8,128)(2,1)S(1)}, u32[]{:S(2)}, u32[]{:S(2)}) collective-permute-start(bf16[128,512]{1,0:T(8,128)(2,1)S(1)} %get-tuple-element.171), channel_id=1, source_target_pairs={{0,4},{4,8},{8,12},{12,16},{16,20},{20,24},{24,28},{28,32},{32,36}... | collective-permute-start | bytes 393224 | tf_op jit(solution)/shard_map/while/body/eval_jaxpr/ppermute | solution.py:14
  855.1 11.8 %collective-permute-start.1 = (s32[128]{0:T(128)S(1)}, s32[128]{0:T(128)S(1)}, u32[]{:S(2)}, u32[]{:S(2)}) collective-permute-start(s32[128]{0:T(128)S(1)} %get-tuple-element.172), channel_id=1, source_target_pairs={{0,4},{4,8},{8,12},{12,16},{16,20},{20,24},{24,28},{28,32},{32,36}... | collective-permute-start | bytes 1544 | tf_op jit(solution)/shard_map/while/body/eval_jaxpr/ppermute | solution.py:14
  867.0 13.8 %collective-permute-start = (bf16[128,512]{1,0:T(8,128)(2,1)S(1)}, bf16[128,512]{1,0:T(8,128)(2,1)S(1)}, u32[]{:S(2)}, u32[]{:S(2)}) collective-permute-start(bf16[128,512]{1,0:T(8,128)(2,1)S(1)} %get-tuple-element.171), channel_id=1, source_target_pairs={{0,4},{4,8},{8,12},{12,16},{16,20},{20,24},{24,28},{28,32},{32,36}... | collective-permute-start | bytes 393224 | tf_op jit(solution)/shard_map/while/body/eval_jaxpr/ppermute | solution.py:14
  869.0 11.9 %collective-permute-start.1 = (s32[128]{0:T(128)S(1)}, s32[128]{0:T(128)S(1)}, u32[]{:S(2)}, u32[]{:S(2)}) collective-permute-start(s32[128]{0:T(128)S(1)} %get-tuple-element.172), channel_id=1, source_target_pairs={{0,4},{4,8},{8,12},{12,16},{16,20},{20,24},{24,28},{28,32},{32,36}... | collective-permute-start | bytes 1544 | tf_op jit(solution)/shard_map/while/body/eval_jaxpr/ppermute | solution.py:14
  880.9 14.7 %collective-permute-start = (bf16[128,512]{1,0:T(8,128)(2,1)S(1)}, bf16[128,512]{1,0:T(8,128)(2,1)S(1)}, u32[]{:S(2)}, u32[]{:S(2)}) collective-permute-start(bf16[128,512]{1,0:T(8,128)(2,1)S(1)} %get-tuple-element.171), channel_id=1, source_target_pairs={{0,4},{4,8},{8,12},{12,16},{16,20},{20,24},{24,28},{28,32},{32,36}... | collective-permute-start | bytes 393224 | tf_op jit(solution)/shard_map/while/body/eval_jaxpr/ppermute | solution.py:14
  882.8 12.8 %collective-permute-start.1 = (s32[128]{0:T(128)S(1)}, s32[128]{0:T(128)S(1)}, u32[]{:S(2)}, u32[]{:S(2)}) collective-permute-start(s32[128]{0:T(128)S(1)} %get-tuple-element.172), channel_id=1, source_target_pairs={{0,4},{4,8},{8,12},{12,16},{16,20},{20,24},{24,28},{28,32},{32,36}... | collective-permute-start | bytes 1544 | tf_op jit(solution)/shard_map/while/body/eval_jaxpr/ppermute | solution.py:14
  895.7 13.8 %collective-permute-start = (bf16[128,512]{1,0:T(8,128)(2,1)S(1)}, bf16[128,512]{1,0:T(8,128)(2,1)S(1)}, u32[]{:S(2)}, u32[]{:S(2)}) collective-permute-start(bf16[128,512]{1,0:T(8,128)(2,1)S(1)} %get-tuple-element.171), channel_id=1, source_target_pairs={{0,4},{4,8},{8,12},{12,16},{16,20},{20,24},{24,28},{28,32},{32,36}... | collective-permute-start | bytes 393224 | tf_op jit(solution)/shard_map/while/body/eval_jaxpr/ppermute | solution.py:14
  897.6 11.8 %collective-permute-start.1 = (s32[128]{0:T(128)S(1)}, s32[128]{0:T(128)S(1)}, u32[]{:S(2)}, u32[]{:S(2)}) collective-permute-start(s32[128]{0:T(128)S(1)} %get-tuple-element.172), channel_id=1, source_target_pairs={{0,4},{4,8},{8,12},{12,16},{16,20},{20,24},{24,28},{28,32},{32,36}... | collective-permute-start | bytes 1544 | tf_op jit(solution)/shard_map/while/body/eval_jaxpr/ppermute | solution.py:14
  909.5 13.8 %collective-permute-start = (bf16[128,512]{1,0:T(8,128)(2,1)S(1)}, bf16[128,512]{1,0:T(8,128)(2,1)S(1)}, u32[]{:S(2)}, u32[]{:S(2)}) collective-permute-start(bf16[128,512]{1,0:T(8,128)(2,1)S(1)} %get-tuple-element.171), channel_id=1, source_target_pairs={{0,4},{4,8},{8,12},{12,16},{16,20},{20,24},{24,28},{28,32},{32,36}... | collective-permute-start | bytes 393224 | tf_op jit(solution)/shard_map/while/body/eval_jaxpr/ppermute | solution.py:14
  923.3 13.8 %collective-permute-start = (bf16[128,512]{1,0:T(8,128)(2,1)S(1)}, bf16[128,512]{1,0:T(8,128)(2,1)S(1)}, u32[]{:S(2)}, u32[]{:S(2)}) collective-permute-start(bf16[128,512]{1,0:T(8,128)(2,1)S(1)} %get-tuple-element.171), channel_id=1, source_target_pairs={{0,4},{4,8},{8,12},{12,16},{16,20},{20,24},{24,28},{28,32},{32,36}... | collective-permute-start | bytes 393224 | tf_op jit(solution)/shard_map/while/body/eval_jaxpr/ppermute | solution.py:14
  925.3 11.8 %collective-permute-start.1 = (s32[128]{0:T(128)S(1)}, s32[128]{0:T(128)S(1)}, u32[]{:S(2)}, u32[]{:S(2)}) collective-permute-start(s32[128]{0:T(128)S(1)} %get-tuple-element.172), channel_id=1, source_target_pairs={{0,4},{4,8},{8,12},{12,16},{16,20},{20,24},{24,28},{28,32},{32,36}... | collective-permute-start | bytes 1544 | tf_op jit(solution)/shard_map/while/body/eval_jaxpr/ppermute | solution.py:14
  937.2 13.8 %collective-permute-start = (bf16[128,512]{1,0:T(8,128)(2,1)S(1)}, bf16[128,512]{1,0:T(8,128)(2,1)S(1)}, u32[]{:S(2)}, u32[]{:S(2)}) collective-permute-start(bf16[128,512]{1,0:T(8,128)(2,1)S(1)} %get-tuple-element.171), channel_id=1, source_target_pairs={{0,4},{4,8},{8,12},{12,16},{16,20},{20,24},{24,28},{28,32},{32,36}... | collective-permute-start | bytes 393224 | tf_op jit(solution)/shard_map/while/body/eval_jaxpr/ppermute | solution.py:14
  951.0 13.8 %collective-permute-start = (bf16[128,512]{1,0:T(8,128)(2,1)S(1)}, bf16[128,512]{1,0:T(8,128)(2,1)S(1)}, u32[]{:S(2)}, u32[]{:S(2)}) collective-permute-start(bf16[128,512]{1,0:T(8,128)(2,1)S(1)} %get-tuple-element.171), channel_id=1, source_target_pairs={{0,4},{4,8},{8,12},{12,16},{16,20},{20,24},{24,28},{28,32},{32,36}... | collective-permute-start | bytes 393224 | tf_op jit(solution)/shard_map/while/body/eval_jaxpr/ppermute | solution.py:14
  952.9 11.8 %collective-permute-start.1 = (s32[128]{0:T(128)S(1)}, s32[128]{0:T(128)S(1)}, u32[]{:S(2)}, u32[]{:S(2)}) collective-permute-start(s32[128]{0:T(128)S(1)} %get-tuple-element.172), channel_id=1, source_target_pairs={{0,4},{4,8},{8,12},{12,16},{16,20},{20,24},{24,28},{28,32},{32,36}... | collective-permute-start | bytes 1544 | tf_op jit(solution)/shard_map/while/body/eval_jaxpr/ppermute | solution.py:14
  964.8 13.8 %collective-permute-start = (bf16[128,512]{1,0:T(8,128)(2,1)S(1)}, bf16[128,512]{1,0:T(8,128)(2,1)S(1)}, u32[]{:S(2)}, u32[]{:S(2)}) collective-permute-start(bf16[128,512]{1,0:T(8,128)(2,1)S(1)} %get-tuple-element.171), channel_id=1, source_target_pairs={{0,4},{4,8},{8,12},{12,16},{16,20},{20,24},{24,28},{28,32},{32,36}... | collective-permute-start | bytes 393224 | tf_op jit(solution)/shard_map/while/body/eval_jaxpr/ppermute | solution.py:14
  978.6 13.8 %collective-permute-start = (bf16[128,512]{1,0:T(8,128)(2,1)S(1)}, bf16[128,512]{1,0:T(8,128)(2,1)S(1)}, u32[]{:S(2)}, u32[]{:S(2)}) collective-permute-start(bf16[128,512]{1,0:T(8,128)(2,1)S(1)} %get-tuple-element.171), channel_id=1, source_target_pairs={{0,4},{4,8},{8,12},{12,16},{16,20},{20,24},{24,28},{28,32},{32,36}... | collective-permute-start | bytes 393224 | tf_op jit(solution)/shard_map/while/body/eval_jaxpr/ppermute | solution.py:14
  980.6 11.8 %collective-permute-start.1 = (s32[128]{0:T(128)S(1)}, s32[128]{0:T(128)S(1)}, u32[]{:S(2)}, u32[]{:S(2)}) collective-permute-start(s32[128]{0:T(128)S(1)} %get-tuple-element.172), channel_id=1, source_target_pairs={{0,4},{4,8},{8,12},{12,16},{16,20},{20,24},{24,28},{28,32},{32,36}... | collective-permute-start | bytes 1544 | tf_op jit(solution)/shard_map/while/body/eval_jaxpr/ppermute | solution.py:14
  992.5 13.8 %collective-permute-start = (bf16[128,512]{1,0:T(8,128)(2,1)S(1)}, bf16[128,512]{1,0:T(8,128)(2,1)S(1)}, u32[]{:S(2)}, u32[]{:S(2)}) collective-permute-start(bf16[128,512]{1,0:T(8,128)(2,1)S(1)} %get-tuple-element.171), channel_id=1, source_target_pairs={{0,4},{4,8},{8,12},{12,16},{16,20},{20,24},{24,28},{28,32},{32,36}... | collective-permute-start | bytes 393224 | tf_op jit(solution)/shard_map/while/body/eval_jaxpr/ppermute | solution.py:14
  (14 other events, 2502.9 us)
Sparse Core Ops, SparseCore 0:
  12.7 135.0 all-gather.7
  152.5 127.5 all-gather.9
  284.8 127.3 all-gather.11
  1015.8 31.6 reduce-scatter.3
